TPU v7x, 512 devices: a whole 4x8x8 slice. The times are simulated.
512 devices in a mesh: expert: 32 (over y, z_hi, core), tensor: 4 (over x), dp: 4 (over z_lo).
Axes of the slice: x: 4, y: 8, z: 8 (z_hi: 2, z_lo: 4; z = z_hi * 4 + z_lo), core: 2. Of those that a mesh axis runs over, the one named last changes fastest.
Arguments:
- tokens: bfloat16 [16384, 4096], P(('expert', 'dp'), 'tensor'), may hold values from -6 to 6
- routes: int32 [16384, 2], P(('expert', 'dp')), may hold values from 0 to 31, all different within a row; in each aligned block of 128 rows (0 to 127, 128 to 255, ...) at most 10 rows name the same one
- gate_prob: float32 [16384, 2], P(('expert', 'dp')), may hold values from 0.05 to 1
- token_count: int32 [128], P(('expert', 'dp')), may hold values from 1 to 128, 12288 in all
- gate_weight: bfloat16 [32, 4096, 1536], P(None, ('expert', 'dp'), 'tensor'), may hold values from -0.09375 to 0.09375
- up_weight: bfloat16 [32, 4096, 1536], P(None, ('expert', 'dp'), 'tensor'), may hold values from -0.09375 to 0.09375
- down_weight: bfloat16 [32, 4096, 1536], P(None, ('expert', 'dp'), 'tensor'), may hold values from -0.15625 to 0.15625
Outputs:
- mixed: bfloat16 [16384, 4096], P(('expert', 'dp'), 'tensor')
Inputs may be any that keep to these rules, and one draw needn't show every extreme that they name: `routes`: each row names 2 different experts; among the rows of one group (aligned blocks of 128 rows) no expert is named by more than 10 rows. `token_count`: rows of a group at or past its count are padding.
All inputs are finite; a program needn't handle non-finite values.
Results may differ from a plain program's by a relative error of at most 0.012.
Values may be sent and summed in bfloat16 or wider, within the bound.
A program may use at most 64 MiB of HBM per device.

v0:
```python
import jax
import jax.numpy as jnp
from jax import lax
from jax.sharding import PartitionSpec as P


def shards(tokens, routes, gate_prob, token_count, gate_weight, up_weight, down_weight):
    experts = gate_weight.shape[0]
    stored_rows = gate_weight.shape[1]
    hidden_share = gate_weight.shape[2]
    tok_rows, top_slots = routes.shape
    capacity = min(tok_rows, tok_rows * top_slots * 5 // (4 * experts))
    expert_count = lax.axis_size("expert")
    replica_count = lax.axis_size("dp")
    model_width = stored_rows * expert_count * replica_count
    arrived_rows = (
        lax.all_to_all(gate_weight, "expert", split_axis=0, concat_axis=1, tiled=True),
        lax.all_to_all(up_weight, "expert", split_axis=0, concat_axis=1, tiled=True),
        lax.all_to_all(down_weight, "expert", split_axis=0, concat_axis=1, tiled=True),
    )

    def split_blocks(weight):
        return weight.reshape(1, expert_count, 1, stored_rows, hidden_share)

    assembled = (
        lax.all_gather(split_blocks(arrived_rows[0]), "dp", axis=2, tiled=True),
        lax.all_gather(split_blocks(arrived_rows[1]), "dp", axis=2, tiled=True),
        lax.all_gather(split_blocks(arrived_rows[2]), "dp", axis=2, tiled=True),
    )
    w_gate = assembled[0].reshape(model_width, hidden_share)
    w_up = assembled[1].reshape(model_width, hidden_share)
    w_down = assembled[2].reshape(model_width, hidden_share)
    positions = jnp.arange(tok_rows)
    live_rows = positions < token_count[0]
    live_pair = jnp.repeat(live_rows, top_slots)
    route_flat = routes.reshape(-1)
    expert_ids = jnp.arange(experts)
    one_hot = ((route_flat[:, None] == expert_ids[None, :]) & live_pair[:, None]).astype(jnp.int32)
    pair_rank = jnp.sum((jnp.cumsum(one_hot, axis=0) - one_hot) * one_hot, axis=1)
    slot_of_pair = jnp.where(live_pair, route_flat * capacity + pair_rank, -1)
    slot_ids = jnp.arange(experts * capacity)
    assign_pair = (slot_ids[:, None] == slot_of_pair[None, :]).astype(jnp.bfloat16)
    assign_slots = assign_pair.reshape(experts * capacity, tok_rows, top_slots)
    assign_bf16 = jnp.sum(assign_slots.astype(jnp.float32), axis=2).astype(jnp.bfloat16)
    outgoing = jnp.dot(assign_bf16, tokens, preferred_element_type=jnp.float32).astype(jnp.bfloat16)
    incoming = lax.all_to_all(
        outgoing.reshape(experts, capacity, tokens.shape[1]),
        "expert",
        split_axis=0,
        concat_axis=0,
        tiled=True,
    )
    feature_piece = lax.all_gather(incoming, "tensor", axis=2, tiled=True)
    piece_width = feature_piece.shape[2]
    flat_piece = feature_piece.reshape(-1, piece_width)
    gate_proj = jnp.dot(flat_piece, w_gate, preferred_element_type=jnp.float32)
    up_proj = jnp.dot(flat_piece, w_up, preferred_element_type=jnp.float32)
    hidden = (jax.nn.silu(gate_proj) * up_proj).astype(jnp.bfloat16)
    partial_value = lax.dot_general(
        hidden, w_down, (((1,), (1,)), ((), ())), preferred_element_type=jnp.float32
    )
    expert_out = lax.psum_scatter(
        partial_value.astype(jnp.bfloat16), "tensor", scatter_dimension=1, tiled=True
    )
    returned = lax.all_to_all(
        expert_out.reshape(experts, capacity, -1), "expert", split_axis=0, concat_axis=0, tiled=True
    )
    returned_rows = returned.reshape(experts * capacity, -1)
    picked = jnp.einsum(
        "cts,cd->std", assign_slots, returned_rows, preferred_element_type=jnp.float32
    )
    slot_weights = gate_prob.T
    mixed = jnp.sum(slot_weights[:, :, None] * picked, axis=0)
    return mixed.astype(jnp.bfloat16)


def solution(mesh):
    in_specs = (
        P(("expert", "dp"), "tensor"),
        P(("expert", "dp"), None),
        P(("expert", "dp"), None),
        P(("expert", "dp")),
        P(None, ("expert", "dp"), "tensor"),
        P(None, ("expert", "dp"), "tensor"),
        P(None, ("expert", "dp"), "tensor"),
    )
    out_specs = P(("expert", "dp"), "tensor")
    return jax.shard_map(shards, mesh=mesh, in_specs=in_specs, out_specs=out_specs, check_vma=False)
```

profile of v0, /device:TPU:1, one launch (start us, length us, event | category | flops | bytes accessed | tf_op | source)
XLA Modules:
  0.0 439.4 jit_solution(14603103869681247513)
XLA Ops:
  6.5 0.0 copy-start
  6.5 0.0 all-gather.8.cloned.1.call-start
  6.5 0.8 copy.30
  7.4 0.1 eq.66
  7.5 0.1 eq.62
  8.3 0.1 broadcast_in_dim.16
  8.4 0.1 broadcast_in_dim.17
  8.6 0.0 copy-start.1
  8.6 0.6 reduce-window.6
  9.2 0.2 slice_reduce_fusion
  9.4 0.1 broadcast_in_dim.15.clone
  9.5 0.1 and.16
  9.7 0.1 fusion.16
  9.8 0.1 reduce_sum.33
  9.9 0.1 copy.34
  10.0 0.7 add_select_fusion
  10.7 0.0 copy-done
  10.7 0.3 convolution_convert_fusion.1
  11.1 0.2 reshape.115
  11.3 0.0 copy-start.2
  11.3 47.6 %all_to_all.37 = bf16[32,10,1024]{2,1,0:T(8,128)(2,1)} all-to-all(bf16[32,10,1024]{2,1,0:T(8,128)(2,1)S(1)} %reshape.115), channel_id=1, replica_groups=mesh['expert'=32,'tensor'=4,'dp'=4] {'expert'}, dimensions={0} | all-to-all | bytes 1310720 | tf_op jit(solution)/shard_map/all_to_all | solution.py:46
  58.9 0.0 copy-start.3
  58.9 0.0 all-gather.8.cloned.1.call-update
  58.9 0.0 all-gather.10.cloned.1.call-start
  58.9 0.0 copy-done.1
  59.0 31.1 %all_to_all.38 = bf16[32,32,384]{2,1,0:T(8,128)(2,1)} all-to-all(bf16[32,32,384]{2,1,0:T(8,128)(2,1)S(1)} %copy-done.1), channel_id=1, replica_groups=mesh['expert'=32,'tensor'=4,'dp'=4] {'expert'}, dimensions={0} | all-to-all | bytes 1572864 | tf_op jit(solution)/shard_map/all_to_all | solution.py:17
  90.0 0.0 all-gather.10.cloned.1.call-update
  90.0 0.0 all-gather.12.cloned.1.call-start
  90.1 0.0 copy-done.2
  90.1 30.9 %all_to_all.39 = bf16[32,32,384]{2,1,0:T(8,128)(2,1)} all-to-all(bf16[32,32,384]{2,1,0:T(8,128)(2,1)S(1)} %copy-done.2), channel_id=1, replica_groups=mesh['expert'=32,'tensor'=4,'dp'=4] {'expert'}, dimensions={0} | all-to-all | bytes 1572864 | tf_op jit(solution)/shard_map/all_to_all | solution.py:18
  121.0 0.0 all-gather.12.cloned.1.call-update
  121.0 0.0 all-gather.14.cloned.1.call-start
  121.0 0.0 copy-done.3
  121.0 30.7 %all_to_all.40 = bf16[32,32,384]{2,1,0:T(8,128)(2,1)} all-to-all(bf16[32,32,384]{2,1,0:T(8,128)(2,1)S(1)} %copy-done.3), channel_id=1, replica_groups=mesh['expert'=32,'tensor'=4,'dp'=4] {'expert'}, dimensions={0} | all-to-all | bytes 1572864 | tf_op jit(solution)/shard_map/all_to_all | solution.py:19
  151.8 0.0 all-gather.14.cloned.1.call-update
  151.8 0.0 reduce-scatter.2.cloned.1.call-start
  151.9 0.0 all-gather.8.cloned.1.call-done
  151.9 3.3 reshape.116
  155.2 41.5 %all-gather.10.cloned.1.call-done = bf16[32,128,384]{2,1,0:T(8,128)(2,1)} async-done(((bf16[32,32,384]{2,1,0:T(8,128)(2,1)}), bf16[32,128,384]{2,1,0:T(8,128)(2,1)}) %all-gather.10.cloned.1.call-update) | async-done | bytes 3145744 | tf_op jit(solution)/shard_map/all_gather | solution.py:26
  196.7 3.4 fusion.21
  200.1 68.5 %all-gather.12.cloned.1.call-done = bf16[32,128,384]{2,1,0:T(8,128)(2,1)} async-done(((bf16[32,32,384]{2,1,0:T(8,128)(2,1)}), bf16[32,128,384]{2,1,0:T(8,128)(2,1)}) %all-gather.12.cloned.1.call-update) | async-done | bytes 3145744 | tf_op jit(solution)/shard_map/all_gather | solution.py:27
  268.7 71.8 %all-gather.14.cloned.1.call-done = bf16[32,128,384]{2,1,0:T(8,128)(2,1)} async-done(((bf16[32,32,384]{2,1,0:T(8,128)(2,1)}), bf16[32,128,384]{2,1,0:T(8,128)(2,1)}) %all-gather.14.cloned.1.call-update) | async-done | bytes 3145744 | tf_op jit(solution)/shard_map/all_gather | solution.py:28
  340.5 7.3 %convolution_convert_fusion = bf16[320,4096]{1,0:T(8,128)(2,1)} fusion(bf16[4096,384]{1,0:T(8,128)(2,1)} %bitcast.45, bf16[320,4096]{1,0:T(8,128)(2,1)S(1)} %reshape.116, bf16[4096,384]{1,0:T(8,128)(2,1)} %bitcast.44, f32[320,384]{1,0:T(8,128)S(1)} %fusion.21), kind=kOutput, calls=%fused_computation | convolution fusion | flops 2015313920 | bytes 12025856 | tf_op jit(solution)/shard_map/dot_general | solution.py:59
  347.8 0.0 reduce-scatter.2.cloned.1.call-update
  347.8 0.0 copy-start.4
  347.8 39.7 %reduce-scatter.2.cloned.1.call-done = bf16[320,1024]{1,0:T(8,128)(2,1)} async-done(((bf16[320,4096]{1,0:T(8,128)(2,1)}), bf16[320,1024]{1,0:T(8,128)(2,1)}) %reduce-scatter.2.cloned.1.call-update) | async-done | bytes 655376 | tf_op jit(solution)/shard_map/reduce_scatter | solution.py:62
  387.5 1.3 reshape.123
  388.8 42.5 %all_to_all.41 = bf16[32,10,1024]{2,1,0:T(8,128)(2,1)S(1)} all-to-all(bf16[32,10,1024]{2,1,0:T(8,128)(2,1)S(1)} %reshape.123), channel_id=1, replica_groups=mesh['expert'=32,'tensor'=4,'dp'=4] {'expert'}, dimensions={0} | all-to-all | bytes 1310720 | tf_op jit(solution)/shard_map/all_to_all | solution.py:65
  431.3 0.2 reshape.131
  431.5 0.0 copy-done.4
  431.5 0.5 fusion.1
  432.0 0.9 copy.35
  (6 shorter events, 0.1 us)
Async XLA Ops:
  6.5 4.2 copy-start
  6.5 145.3 %all-gather.8.cloned.1.call-start = ((), (), s32[]{:S(2)}) async-start(), calls=%async_computation.6 | async-start | bytes 5242880 | tf_op jit(solution)/shard_map/all_gather | solution.py:53
  8.6 50.4 %copy-start.1 = (bf16[32,32,384]{2,1,0:T(8,128)(2,1)S(1)}, bf16[32,32,384]{2,1,0:T(8,128)(2,1)}, u32[]{:S(2)}) copy-start(bf16[32,32,384]{2,1,0:T(8,128)(2,1)} %param.11) | copy-start | bytes 2359300
  11.3 78.8 %copy-start.2 = (bf16[32,32,384]{2,1,0:T(8,128)(2,1)S(1)}, bf16[32,32,384]{2,1,0:T(8,128)(2,1)}, u32[]{:S(2)}) copy-start(bf16[32,32,384]{2,1,0:T(8,128)(2,1)} %param.12) | copy-start | bytes 2359300
  58.9 62.2 %copy-start.3 = (bf16[32,32,384]{2,1,0:T(8,128)(2,1)S(1)}, bf16[32,32,384]{2,1,0:T(8,128)(2,1)}, u32[]{:S(2)}) copy-start(bf16[32,32,384]{2,1,0:T(8,128)(2,1)} %param.13) | copy-start | bytes 2359300
  58.9 137.8 %all-gather.10.cloned.1.call-start = ((), (), s32[]{:S(2)}) async-start(), calls=%async_computation.8 | async-start | bytes 3932160 | tf_op jit(solution)/shard_map/all_gather | solution.py:26
  90.0 178.6 %all-gather.12.cloned.1.call-start = ((), (), s32[]{:S(2)}) async-start(), calls=%async_computation.9 | async-start | bytes 3932160 | tf_op jit(solution)/shard_map/all_gather | solution.py:27
  121.0 219.5 %all-gather.14.cloned.1.call-start = ((), (), s32[]{:S(2)}) async-start(), calls=%async_computation.10 | async-start | bytes 3932160 | tf_op jit(solution)/shard_map/all_gather | solution.py:28
  151.8 235.7 %reduce-scatter.2.cloned.1.call-start = ((), (), s32[]{:S(2)}) async-start(), calls=%async_computation.7 | async-start | bytes 3276800 | tf_op jit(solution)/shard_map/reduce_scatter | solution.py:62
  347.8 83.7 %copy-start.4 = (f32[128,2]{0,1:T(2,128)S(1)}, f32[128,2]{0,1:T(2,128)}, u32[]{:S(2)}) copy-start(f32[128,2]{0,1:T(2,128)} %param.9) | copy-start | bytes 3076
Sparse Core Ops, SparseCore 0:
  59.0 49.7 all-gather.7
  110.9 85.8 all-gather.9
  198.8 69.7 all-gather.11
  270.6 69.7 all-gather.13
  347.9 39.5 reduce-scatter.1
where the time goes:
time: 440 us; the launch traced here: 439 us
  waiting for transfers between devices  222 us (50%)
  blocking collectives  183 us (42%)
  between operations  14 us (3%)
  matrix products  11.5 us (3%)
  local copies, waits for them, and re-layouts  7.87 us (2%)
    all_gather x1, waiting for transfers between devices, shards(): lax.all_gather(split_blocks(arrived_rows[2]), 'dp', axis=2, tiled=True)  71.8 us
    all_gather x1, waiting for transfers between devices, shards(): lax.all_gather(split_blocks(arrived_rows[1]), 'dp', axis=2, tiled=True)  68.5 us
    all_to_all x1, blocking collectives, shards(): lax.all_to_all(outgoing.reshape(experts, capacity, tokens.shape[1]), 'exp...  47.6 us
    all_to_all x1, blocking collectives, shards(): lax.all_to_all(expert_out.reshape(experts, capacity, -1), 'expert', split...  42.5 us
    all_gather x1, waiting for transfers between devices, shards(): lax.all_gather(split_blocks(arrived_rows[0]), 'dp', axis=2, tiled=True)  41.5 us
    reduce_scatter x1, waiting for transfers between devices, shards(): lax.psum_scatter(partial_value.astype(jnp.bfloat16), 'tensor', scatter_di...  39.7 us
    all_to_all x1, blocking collectives, shards(): lax.all_to_all(gate_weight, 'expert', split_axis=0, concat_axis=1, tiled=...  31.1 us
    all_to_all x1, blocking collectives, shards(): lax.all_to_all(up_weight, 'expert', split_axis=0, concat_axis=1, tiled=True)  30.9 us
  transfers between devices with their start and end apart: 5, of which 4 were waited for; matrix products, arithmetic and copies ran while one was open for 2% of the time, Pallas kernels for 0%

commit v1 on v0

--- a/solution.py
+++ b/solution.py
@@ -2,6 +2,13 @@
 import jax.numpy as jnp
 from jax import lax
 from jax.sharding import PartitionSpec as P
+
+
+def all_by_exchange(x, name, dim):
+    size = lax.axis_size(name)
+    blocks = jnp.stack([x for _ in range(size)])
+    blocks = lax.all_to_all(blocks, name, split_axis=0, concat_axis=0)
+    return jnp.concatenate(blocks, axis=dim)
 
 
 def shards(tokens, routes, gate_prob, token_count, gate_weight, up_weight, down_weight):
@@ -23,7 +30,7 @@
         return weight.reshape(1, expert_count, 1, stored_rows, hidden_share)
 
     assembled = (
-        lax.all_gather(split_blocks(arrived_rows[0]), "dp", axis=2, tiled=True),
+        all_by_exchange(split_blocks(arrived_rows[0]), "dp", 2),
         lax.all_gather(split_blocks(arrived_rows[1]), "dp", axis=2, tiled=True),
         lax.all_gather(split_blocks(arrived_rows[2]), "dp", axis=2, tiled=True),
     )

time: 440 us -> 421 us (0.957)
  waiting for transfers between devices: 222 us -> 196 us
  local copies, waits for them, and re-layouts: 7.87 us -> 13.1 us
    all_to_all x0 -> x1, waiting for transfers between devices: none -> 102 us  [all_by_exchange(): blocks = lax.all_to_all(blocks, name, split_axis=0, concat_axis=0)]
    all_gather x1, waiting for transfers between devices: 68.5 us -> 0.02 us  [shards(): lax.all_gather(split_blocks(arrived_rows[1]), 'dp', axis=2, tiled=True)]
    all_gather x1 -> x0, waiting for transfers between devices: 41.5 us -> none  [shards(): lax.all_gather(split_blocks(arrived_rows[0]), 'dp', axis=2, tiled=True)]
    all_gather x1, waiting for transfers between devices: 71.8 us -> 53.2 us  [shards(): lax.all_gather(split_blocks(arrived_rows[2]), 'dp', axis=2, tiled=True)]
  transfers between devices with their start and end apart: 5 -> 5, of which waited for: 4 -> 3; matrix products, arithmetic and copies ran while one was open for 2% -> 2% of each run, Pallas kernels for 0% -> 0%
where the time goes in v1:
time: 421 us
  waiting for transfers between devices  196 us (47%)
  blocking collectives  183 us (43%)
  between operations  14 us (3%)
  local copies, waits for them, and re-layouts  13.1 us (3%)
  matrix products  9.65 us (2%)
    all_to_all x1, waiting for transfers between devices, all_by_exchange(): blocks = lax.all_to_all(blocks, name, split_axis=0, concat_axis=0)  102 us
    all_gather x1, waiting for transfers between devices, shards(): lax.all_gather(split_blocks(arrived_rows[2]), 'dp', axis=2, tiled=True)  53.2 us
    all_to_all x1, blocking collectives, shards(): lax.all_to_all(outgoing.reshape(experts, capacity, tokens.shape[1]), 'exp...  47.6 us
    all_to_all x1, blocking collectives, shards(): lax.all_to_all(expert_out.reshape(experts, capacity, -1), 'expert', split...  42.5 us
    reduce_scatter x1, waiting for transfers between devices, shards(): lax.psum_scatter(partial_value.astype(jnp.bfloat16), 'tensor', scatter_di...  39.7 us
    all_to_all x1, blocking collectives, shards(): lax.all_to_all(up_weight, 'expert', split_axis=0, concat_axis=1, tiled=True)  31.1 us
    all_to_all x1, blocking collectives, shards(): lax.all_to_all(gate_weight, 'expert', split_axis=0, concat_axis=1, tiled=...  30.8 us
    all_to_all x1, blocking collectives, shards(): lax.all_to_all(down_weight, 'expert', split_axis=0, concat_axis=1, tiled=...  30.7 us
  transfers between devices with their start and end apart: 5, of which 3 were waited for; matrix products, arithmetic and copies ran while one was open for 2% of the time, Pallas kernels for 0%

profile of v1, /device:TPU:1, one launch (start us, length us, event | category | flops | bytes accessed | tf_op | source)
XLA Modules:
  0.0 420.8 jit_solution(10964825765243975783)
XLA Ops:
  6.5 0.0 copy-start
  6.5 0.0 all-gather.6.cloned.1.call-start
  6.5 0.8 copy.32
  7.4 0.1 eq.66
  7.5 0.1 eq.62
  8.3 0.1 broadcast_in_dim.16
  8.4 0.1 broadcast_in_dim.17
  8.6 0.0 copy-start.3
  8.6 0.6 reduce-window.6
  9.2 0.2 slice_reduce_fusion
  9.4 0.1 broadcast_in_dim.15.clone
  9.5 0.1 and.16
  9.7 0.1 fusion.16
  9.8 0.1 reduce_sum.33
  9.9 0.1 copy.36
  10.0 0.7 add_select_fusion
  10.7 0.0 copy-done
  10.7 0.3 convolution_convert_fusion.1
  11.1 0.2 reshape.114
  11.3 0.0 copy-start.4
  11.3 47.6 %all_to_all.42 = bf16[32,10,1024]{2,1,0:T(8,128)(2,1)} all-to-all(bf16[32,10,1024]{2,1,0:T(8,128)(2,1)S(1)} %reshape.114), channel_id=1, replica_groups=mesh['expert'=32,'tensor'=4,'dp'=4] {'expert'}, dimensions={0} | all-to-all | bytes 1310720 | tf_op jit(solution)/shard_map/all_to_all | solution.py:53
  58.9 0.0 copy-start.5
  58.9 0.0 all-gather.6.cloned.1.call-update
  58.9 0.0 all-gather.8.cloned.1.call-start
  58.9 0.0 copy-done.3
  59.0 31.1 %all_to_all.43 = bf16[32,32,384]{2,1,0:T(8,128)(2,1)} all-to-all(bf16[32,32,384]{2,1,0:T(8,128)(2,1)S(1)} %copy-done.3), channel_id=1, replica_groups=mesh['expert'=32,'tensor'=4,'dp'=4] {'expert'}, dimensions={0} | all-to-all | bytes 1572864 | tf_op jit(solution)/shard_map/all_to_all | solution.py:25
  90.0 0.0 all-gather.8.cloned.1.call-update
  90.0 0.0 copy-done.4
  90.1 30.8 %all_to_all.44 = bf16[32,32,384]{2,1,0:T(8,128)(2,1)S(1)} all-to-all(bf16[32,32,384]{2,1,0:T(8,128)(2,1)S(1)} %copy-done.4), channel_id=1, replica_groups=mesh['expert'=32,'tensor'=4,'dp'=4] {'expert'}, dimensions={0} | all-to-all | bytes 1572864 | tf_op jit(solution)/shard_map/all_to_all | solution.py:24
  120.8 0.0 copy-done.5
  120.8 30.7 %all_to_all.45 = bf16[32,32,384]{2,1,0:T(8,128)(2,1)} all-to-all(bf16[32,32,384]{2,1,0:T(8,128)(2,1)S(1)} %copy-done.5), channel_id=1, replica_groups=mesh['expert'=32,'tensor'=4,'dp'=4] {'expert'}, dimensions={0} | all-to-all | bytes 1572864 | tf_op jit(solution)/shard_map/all_to_all | solution.py:26
  151.5 2.1 stack.3
  153.6 3.7 all-to-all-start.2
  157.3 0.0 all-gather.10.cloned.1.call-start
  157.3 0.7 all-gather.10.cloned.1.call-update
  158.0 0.0 reduce-scatter.2.cloned.1.call-start
  158.1 0.0 all-gather.6.cloned.1.call-done
  158.1 4.7 %reshape.115 = bf16[320,4096]{1,0:T(8,128)(2,1)} reshape(bf16[32,10,4096]{2,1,0:T(8,128)(2,1)} %all-gather.6.cloned.1.call-done) | data formatting | bytes 5242880 | tf_op jit(solution)/shard_map/reshape | solution.py:62
  162.8 102.4 %all-to-all-done.2 = bf16[4,1,32,1,32,384]{5,4,2,3,1,0:T(8,128)(2,1)S(1)} async-done(((bf16[4,1,32,1,32,384]{5,4,2,3,1,0:T(8,128)(2,1)}), bf16[4,1,32,1,32,384]{5,4,2,3,1,0:T(8,128)(2,1)S(1)}, u32[]{:S(2)}, u32[]{:S(2)}) %all-to-all-start.2) | async-done | bytes 3145760 | tf_op jit(solution)/shard_map/all_to_all | solution.py:10
  265.2 0.0 copy-start.1
  265.2 0.6 copy.37
  265.8 1.3 copy-done.1
  267.0 0.0 copy-start.2
  267.0 1.5 fusion.21
  268.6 0.0 all-gather.8.cloned.1.call-done
  268.6 53.2 %all-gather.10.cloned.1.call-done = bf16[32,128,384]{2,1,0:T(8,128)(2,1)} async-done(((bf16[32,32,384]{2,1,0:T(8,128)(2,1)}), bf16[32,128,384]{2,1,0:T(8,128)(2,1)}) %all-gather.10.cloned.1.call-update) | async-done | bytes 3145744 | tf_op jit(solution)/shard_map/all_gather | solution.py:35
  321.8 0.0 copy-done.2
  321.8 7.3 %convolution_convert_fusion = bf16[320,4096]{1,0:T(8,128)(2,1)} fusion(bf16[4096,384]{1,0:T(8,128)(2,1)} %bitcast.47, bf16[320,4096]{1,0:T(8,128)(2,1)S(1)} %copy-done.2, bf16[4096,384]{1,0:T(8,128)(2,1)} %bitcast.46, f32[320,384]{1,0:T(8,128)S(1)} %fusion.21), kind=kOutput, calls=%fused_computation | convolution fusion | flops 2015313920 | bytes 12025856 | tf_op jit(solution)/shard_map/dot_general | solution.py:66
  329.1 0.0 reduce-scatter.2.cloned.1.call-update
  329.2 0.0 copy-start.6
  329.2 39.7 %reduce-scatter.2.cloned.1.call-done = bf16[320,1024]{1,0:T(8,128)(2,1)} async-done(((bf16[320,4096]{1,0:T(8,128)(2,1)}), bf16[320,1024]{1,0:T(8,128)(2,1)}) %reduce-scatter.2.cloned.1.call-update) | async-done | bytes 655376 | tf_op jit(solution)/shard_map/reduce_scatter | solution.py:69
  368.9 1.3 reshape.121
  370.2 42.5 %all_to_all.46 = bf16[32,10,1024]{2,1,0:T(8,128)(2,1)S(1)} all-to-all(bf16[32,10,1024]{2,1,0:T(8,128)(2,1)S(1)} %reshape.121), channel_id=1, replica_groups=mesh['expert'=32,'tensor'=4,'dp'=4] {'expert'}, dimensions={0} | all-to-all | bytes 1310720 | tf_op jit(solution)/shard_map/all_to_all | solution.py:72
  412.7 0.2 reshape.127
  412.9 0.0 copy-done.6
  412.9 0.5 fusion.1
  413.4 0.9 copy.38
  (6 shorter events, 0.1 us)
Async XLA Ops:
  6.5 4.2 copy-start
  6.5 151.5 %all-gather.6.cloned.1.call-start = ((), (), s32[]{:S(2)}) async-start(), calls=%async_computation.7 | async-start | bytes 5242880 | tf_op jit(solution)/shard_map/all_gather | solution.py:60
  8.6 50.4 %copy-start.3 = (bf16[32,32,384]{2,1,0:T(8,128)(2,1)S(1)}, bf16[32,32,384]{2,1,0:T(8,128)(2,1)}, u32[]{:S(2)}) copy-start(bf16[32,32,384]{2,1,0:T(8,128)(2,1)} %param.12) | copy-start | bytes 2359300
  11.3 78.8 %copy-start.4 = (bf16[32,32,384]{2,1,0:T(8,128)(2,1)S(1)}, bf16[32,32,384]{2,1,0:T(8,128)(2,1)}, u32[]{:S(2)}) copy-start(bf16[32,32,384]{2,1,0:T(8,128)(2,1)} %param.11) | copy-start | bytes 2359300
  58.9 62.0 %copy-start.5 = (bf16[32,32,384]{2,1,0:T(8,128)(2,1)S(1)}, bf16[32,32,384]{2,1,0:T(8,128)(2,1)}, u32[]{:S(2)}) copy-start(bf16[32,32,384]{2,1,0:T(8,128)(2,1)} %param.13) | copy-start | bytes 2359300
  58.9 209.7 %all-gather.8.cloned.1.call-start = ((), (), s32[]{:S(2)}) async-start(), calls=%async_computation.9 | async-start | bytes 3932160 | tf_op jit(solution)/shard_map/all_gather | solution.py:34
  153.6 111.6 %all-to-all-start.2 = ((bf16[4,1,32,1,32,384]{5,4,2,3,1,0:T(8,128)(2,1)}), bf16[4,1,32,1,32,384]{5,4,2,3,1,0:T(8,128)(2,1)S(1)}, u32[]{:S(2)}, u32[]{:S(2)}) async-start(bf16[4,1,32,1,32,384]{5,4,2,3,1,0:T(8,128)(2,1)} %stack.3), calls=%async_computation.2 | async-start | bytes 6291456 | tf_op jit(solution)/shard_map/all_to_all | solution.py:10
  157.3 164.5 %all-gather.10.cloned.1.call-start = ((), (), s32[]{:S(2)}) async-start(), calls=%async_computation.10 | async-start | bytes 3932160 | tf_op jit(solution)/shard_map/all_gather | solution.py:35
  158.0 210.9 %reduce-scatter.2.cloned.1.call-start = ((), (), s32[]{:S(2)}) async-start(), calls=%async_computation.8 | async-start | bytes 3276800 | tf_op jit(solution)/shard_map/reduce_scatter | solution.py:69
  265.2 1.9 copy-start.1
  267.0 54.8 %copy-start.2 = (bf16[320,4096]{1,0:T(8,128)(2,1)S(1)}, bf16[320,4096]{1,0:T(8,128)(2,1)}, u32[]{:S(2)}) copy-start(bf16[320,4096]{1,0:T(8,128)(2,1)} %reshape.115) | copy-start | bytes 7864324
  329.2 83.8 %copy-start.6 = (f32[128,2]{0,1:T(2,128)S(1)}, f32[128,2]{0,1:T(2,128)}, u32[]{:S(2)}) copy-start(f32[128,2]{0,1:T(2,128)} %param.9) | copy-start | bytes 3076
Sparse Core Ops, SparseCore 0:
  59.0 49.7 all-gather.5
  110.9 119.3 all-gather.7
  232.3 89.4 all-gather.9
  329.3 39.5 reduce-scatter.1
